TPU v7x, 256 devices: a whole 4x4x8 slice. The times are simulated.
256 devices in a mesh: grp: 4 (over y_lo, core), trk: 64 (over z, x, y_hi).
Axes of the slice: x: 4, y: 4 (y_hi: 2, y_lo: 2; y = y_hi * 2 + y_lo), z: 8, core: 2. Of those that a mesh axis runs over, the one named last changes fastest.
Arguments:
- fields: bfloat16 [256, 512, 512], P('grp', 'trk'), may hold values from -81 to 81
- upstream: bfloat16 [256, 512, 512], P('grp', 'trk'), may hold values from -6 to 6
- ln_gain: float32 [512], replicated, may hold values from 0.1 to 1.9
- weights: bfloat16 [4, 512, 512], P(None, 'grp', 'trk'), may hold values from -8 to 8
Outputs:
- grad_fields: bfloat16 [256, 512, 512], P('grp', 'trk')
- grad_weights: float32 [4, 512, 512], P(None, 'grp', 'trk')
- grad_gain: float32 [512], replicated
All inputs are finite; a program needn't handle non-finite values.
Results may differ from a plain program's by a relative error of at most 0.014.
The roundings to bfloat16 on the way count: a program that leaves them out, or rounds other values in their place, can miss the bound.
Values may be sent and summed in bfloat16 or wider, within the bound.
A program may use at most 64 MiB of HBM per device.

v0:
```python
import jax
import jax.numpy as jnp
from jax import lax
from jax.sharding import PartitionSpec as P

HEADS = 8


def normalize(fields, ln_gain):
    values = fields.astype(jnp.float32)
    row_mean = jnp.mean(values, -1, keepdims=True)
    offset = values - row_mean
    row_var = jnp.mean(offset * offset, -1, keepdims=True)
    inv_std = lax.rsqrt(row_var + 1e-05)
    centred = offset * inv_std
    normed = (centred * ln_gain).astype(jnp.bfloat16)
    return (normed, centred, inv_std)


def project(normed, w_in):
    return [
        jnp.einsum("rti,ij->rtj", normed, w_in[index], preferred_element_type=jnp.float32).astype(
            jnp.bfloat16
        )
        for index in range(3)
    ]


def split_heads(block, heads):
    rows, length, width = block.shape
    return (
        block.reshape(rows, length, heads, width // heads)
        .transpose(0, 2, 1, 3)
        .reshape(rows * heads, length, width // heads)
    )


def merge_heads(block, rows):
    items, length, size = block.shape
    return (
        block.reshape(rows, items // rows, length, size)
        .transpose(0, 2, 1, 3)
        .reshape(rows, length, items // rows * size)
    )


def head_back(members):
    query, keyed, valued, grad_out = members
    scaling = query.shape[-1] ** (-0.5)
    scores = jnp.einsum("qd,kd->qk", query, keyed, preferred_element_type=jnp.float32) * scaling
    row_max = jnp.max(scores, -1, keepdims=True)
    shifted = jnp.exp(scores - row_max)
    attn_prob = shifted / jnp.sum(shifted, -1, keepdims=True)
    prob_low = attn_prob.astype(jnp.bfloat16)
    output = jnp.einsum("qk,kd->qd", prob_low, valued, preferred_element_type=jnp.float32).astype(
        jnp.bfloat16
    )
    dprobs = jnp.einsum("qd,kd->qk", grad_out, valued, preferred_element_type=jnp.float32)
    row_dot = jnp.sum(attn_prob * dprobs, -1, keepdims=True)
    score_grad = (attn_prob * (dprobs - row_dot) * scaling).astype(jnp.bfloat16)
    grad_value = jnp.einsum(
        "qk,qd->kd", prob_low, grad_out, preferred_element_type=jnp.float32
    ).astype(jnp.bfloat16)
    grad_query = jnp.einsum(
        "qk,kd->qd", score_grad, keyed, preferred_element_type=jnp.float32
    ).astype(jnp.bfloat16)
    grad_key = jnp.einsum(
        "qk,qd->kd", score_grad, query, preferred_element_type=jnp.float32
    ).astype(jnp.bfloat16)
    return (output, grad_query, grad_key, grad_value)


def attend_back(query_proj, key_proj, value_proj, upstream_rows, w_out):
    rows = query_proj.shape[0]
    grad_attended = jnp.einsum(
        "rtj,ij->rti", upstream_rows, w_out, preferred_element_type=jnp.float32
    ).astype(jnp.bfloat16)
    pieces = lax.map(
        head_back,
        (
            split_heads(query_proj, HEADS),
            split_heads(key_proj, HEADS),
            split_heads(value_proj, HEADS),
            split_heads(grad_attended, HEADS),
        ),
    )
    return [merge_heads(piece, rows) for piece in pieces]


def input_grad(grad_query, grad_key, grad_value, w_in, centred, inv_std, ln_gain):
    stacked = jnp.stack([grad_query, grad_key, grad_value], 2)
    grad_normed = jnp.einsum("rtcj,cij->rti", stacked, w_in, preferred_element_type=jnp.float32)
    width = grad_normed.shape[-1]
    gain_term = jnp.sum((grad_normed * centred).reshape(-1, width), 0)
    scaled = grad_normed * ln_gain
    branch = inv_std * (
        scaled
        - jnp.mean(scaled, -1, keepdims=True)
        - centred * jnp.mean(scaled * centred, -1, keepdims=True)
    )
    return (branch.astype(jnp.bfloat16), gain_term)


def proj_grads(normed, grad_query, grad_key, grad_value):
    return [
        jnp.einsum("rti,rtj->ij", normed, member, preferred_element_type=jnp.float32)
        for member in (grad_query, grad_key, grad_value)
    ]


def shards(fields, upstream, ln_gain, weights):
    w_part = lax.all_gather(weights, "trk", axis=2, tiled=True)
    w_full = lax.all_gather(w_part, "grp", axis=1, tiled=True)
    w_in = w_full[:3]
    w_out = w_full[3]
    rows_dev, trk_dev, width = fields.shape
    cell_count = rows_dev * lax.axis_size("grp") * trk_dev * lax.axis_size("trk")
    normed, centred, inv_std = normalize(fields, ln_gain)
    query_proj, key_proj, value_proj = project(normed, w_in)
    query_rows, key_rows, value_rows, upstream_rows = (
        lax.all_to_all(query_proj, "trk", split_axis=0, concat_axis=1, tiled=True),
        lax.all_to_all(key_proj, "trk", split_axis=0, concat_axis=1, tiled=True),
        lax.all_to_all(value_proj, "trk", split_axis=0, concat_axis=1, tiled=True),
        lax.all_to_all(upstream, "trk", split_axis=0, concat_axis=1, tiled=True),
    )
    attended, grad_query, grad_key, grad_value = attend_back(
        query_rows, key_rows, value_rows, upstream_rows, w_out
    )
    back_query, back_key, back_value = (
        lax.all_to_all(grad_query, "trk", split_axis=1, concat_axis=0, tiled=True),
        lax.all_to_all(grad_key, "trk", split_axis=1, concat_axis=0, tiled=True),
        lax.all_to_all(grad_value, "trk", split_axis=1, concat_axis=0, tiled=True),
    )
    grad_list = proj_grads(normed, back_query, back_key, back_value)
    branch_cells, gain_term = input_grad(
        back_query, back_key, back_value, w_in, centred, inv_std, ln_gain
    )
    out_grad = jnp.einsum(
        "rti,rtj->ij", attended, upstream_rows, preferred_element_type=jnp.float32
    )
    raw_grad = jnp.stack(grad_list + [out_grad])
    partial_grad = lax.psum_scatter(
        raw_grad.astype(jnp.bfloat16), "grp", scatter_dimension=1, tiled=True
    ).astype(jnp.float32)
    summed_grad = lax.psum_scatter(partial_grad, "trk", scatter_dimension=2, tiled=True)
    gain_sum = lax.psum(gain_term, ("grp", "trk"))
    factor = float(cell_count) ** (-0.5)
    grad_fields = (upstream.astype(jnp.float32) + branch_cells.astype(jnp.float32)).astype(
        jnp.bfloat16
    )
    return (grad_fields, summed_grad * factor, gain_sum * factor)


def solution(mesh):
    in_specs = (P("grp", "trk", None), P("grp", "trk", None), P(), P(None, "grp", "trk"))
    out_specs = (P("grp", "trk", None), P(None, "grp", "trk"), P())
    return jax.shard_map(shards, mesh=mesh, in_specs=in_specs, out_specs=out_specs, check_vma=False)
```

profile of v0, /device:TPU:2, one launch (start us, length us, event | category | flops | bytes accessed | tf_op | source)
XLA Modules:
  0.0 1188.6 jit_solution(13073194801549360445)
XLA Ops:
  8.0 184.0 %all_gather.6 = bf16[4,128,512]{1,0,2:T(4,128)(2,1)S(1)} all-gather(bf16[4,128,8]{1,0,2:T(4,128)(2,1)S(1)} %copy.57), channel_id=1, replica_groups=mesh['grp'=4,'trk'=64] {'trk'}, dimensions={2}, use_global_device_ids=true | all-gather | bytes 532480 | tf_op jit(solution)/shard_map/all_gather | solution.py:112
  193.1 8.9 all-to-all-start.3
  202.5 21.9 %all-gather.2.cloned.1.call-done = bf16[4,512,512]{2,1,0:T(8,128)(2,1)} async-done(((bf16[4,128,512]{2,1,0:T(8,128)(2,1)}), bf16[4,512,512]{2,1,0:T(8,128)(2,1)}) %all-gather.2.cloned.1.call-update) | async-done | bytes 2097168 | tf_op jit(solution)/shard_map/all_gather | solution.py:113
  224.3 2.3 convolution_convert_fusion.8
  226.6 13.0 %all-to-all-start = ((bf16[64,8,512]{2,1,0:T(8,128)(2,1)}), bf16[64,8,512]{2,1,0:T(8,128)(2,1)S(1)}, u32[]{:S(2)}, u32[]{:S(2)}) async-start(bf16[64,8,512]{2,1,0:T(8,128)(2,1)} %convolution_convert_fusion.8), calls=%async_computation | async-start | bytes 1048576 | tf_op jit(solution)/shard_map/all_to_all | solution.py:121
  239.7 2.3 convolution_convert_fusion.7
  242.0 16.4 %all-to-all-done = bf16[64,8,512]{2,1,0:T(8,128)(2,1)S(1)} async-done(((bf16[64,8,512]{2,1,0:T(8,128)(2,1)}), bf16[64,8,512]{2,1,0:T(8,128)(2,1)S(1)}, u32[]{:S(2)}, u32[]{:S(2)}) %all-to-all-start) | async-done | bytes 524320 | tf_op jit(solution)/shard_map/all_to_all | solution.py:121
  258.4 6.5 all-to-all-start.1
  265.0 2.3 convolution_convert_fusion.6
  267.3 15.6 %all-to-all-done.1 = bf16[64,8,512]{2,1,0:T(8,128)(2,1)S(1)} async-done(((bf16[64,8,512]{2,1,0:T(8,128)(2,1)}), bf16[64,8,512]{2,1,0:T(8,128)(2,1)S(1)}, u32[]{:S(2)}, u32[]{:S(2)}) %all-to-all-start.1) | async-done | bytes 524320 | tf_op jit(solution)/shard_map/all_to_all | solution.py:122
  282.9 6.7 all-to-all-start.2
  293.1 2.4 reshape.122
  296.9 9.8 all-to-all-done.2
  306.7 2.4 reshape.124
  309.1 2.3 copy.62
  311.4 60.7 %while.16 = (s32[]{:T(128)}, bf16[8,512,64]{1,2,0:T(8,128)(2,1)}, bf16[8,512,64]{1,2,0:T(8,128)(2,1)}, bf16[8,512,64]{1,2,0:T(8,128)(2,1)}, bf16[8,512,64]{1,2,0...) while((s32[]{:T(128)}, bf16[8,512,64]{1,2,0:T(8,128)(2,1)}, ...), condition=%wide.region_6.7_spmd, body=%wide.region_2.6_spmd.sunk | while | flops 206699008 | bytes 11305061 | solution.py:78
  311.9 1.8 fusion.112
  317.2 1.8 fusion.109
  319.5 1.8 fusion.112
  324.8 1.8 fusion.109
  327.1 1.8 fusion.112
  332.4 1.8 fusion.109
  334.7 1.8 fusion.112
  339.9 1.8 fusion.109
  342.3 1.8 fusion.112
  349.9 1.8 fusion.112
  357.5 1.8 fusion.112
  365.0 1.8 fusion.112
  372.1 2.4 copy.65
  375.1 3.8 reduce.1
  379.9 6.5 all-to-all-start.6
  386.4 2.4 copy.64
  388.8 3.8 reduce.2
  393.6 9.5 all-to-all-done.6
  403.1 6.7 all-to-all-start.5
  409.8 2.4 copy.63
  412.2 3.8 reduce.3
  417.1 2.3 fusion.55
  419.9 6.2 all-to-all-done.5
  426.1 6.6 all-to-all-start.4
  434.4 3.6 reshape.149
  439.5 8.9 all-to-all-done.4
  450.2 2.0 fusion.58
  458.0 21.6 %reduce-scatter.2.cloned.1.call-done = bf16[4,128,512]{2,1,0:T(8,128)(2,1)} async-done(((bf16[4,512,512]{2,1,0:T(8,128)(2,1)}), bf16[4,128,512]{2,1,0:T(8,128)(2,1)}) %reduce-scatter.2.cloned.1.call-update) | async-done | bytes 524304 | tf_op jit(solution)/shard_map/reduce_scatter | solution.py:142
  479.6 2.3 copy.69
  481.9 2.8 fusion.64
  484.8 76.2 %psum.7 = f32[512]{0:T(512)S(1)} all-reduce(f32[512]{0:T(512)S(1)} %get-tuple-element.108), channel_id=1, replica_groups=mesh['grp'=4,'trk'=64] {'grp','trk'}, use_global_device_ids=true, to_apply=%region_12.13 | all-reduce | flops 512 | bytes 4096 | tf_op jit(solution)/shard_map/psum | solution.py:146
  562.8 617.9 %all-reduce.3.cloned.1.call-done = f32[4,128,512]{1,0,2:T(4,128)} async-done(((f32[4,128,512]{1,0,2:T(4,128)}), f32[4,128,512]{1,0,2:T(4,128)}) %all-reduce.3.cloned.1.call-update) | async-done | bytes 1048592
  (112 shorter events, 63.0 us)
Async XLA Ops:
  7.2 194.8 %copy-start = (bf16[64,8,512]{2,1,0:T(8,128)(2,1)S(1)}, bf16[64,8,512]{2,1,0:T(8,128)(2,1)}, u32[]{:S(2)}) copy-start(bf16[64,8,512]{2,1,0:T(8,128)(2,1)} %param.6) | copy-start | bytes 1572868
  7.2 217.1 %all-gather.2.cloned.1.call-start = ((), (), s32[]{:S(2)}) async-start(), calls=%async_computation.8 | async-start | bytes 2621440 | tf_op jit(solution)/shard_map/all_gather | solution.py:113
  8.0 216.3 %copy-start.8 = (f32[512]{0:T(512)S(1)}, f32[512]{0:T(512)}, u32[]{:S(2)}) copy-start(f32[512]{0:T(512)} %param.8) | copy-start | bytes 6148
  193.1 33.6 %all-to-all-start.3 = ((bf16[64,8,512]{2,1,0:T(8,128)(2,1)}), bf16[64,8,512]{2,1,0:T(8,128)(2,1)S(1)}, u32[]{:S(2)}, u32[]{:S(2)}) async-start(bf16[64,8,512]{2,1,0:T(8,128)(2,1)} %param.7), calls=%async_computation.3 | async-start | bytes 1048576 | tf_op jit(solution)/shard_map/all_to_all | solution.py:124
  226.6 31.8 %all-to-all-start = ((bf16[64,8,512]{2,1,0:T(8,128)(2,1)}), bf16[64,8,512]{2,1,0:T(8,128)(2,1)S(1)}, u32[]{:S(2)}, u32[]{:S(2)}) async-start(bf16[64,8,512]{2,1,0:T(8,128)(2,1)} %convolution_convert_fusion.8), calls=%async_computation | async-start | bytes 1048576 | tf_op jit(solution)/shard_map/all_to_all | solution.py:121
  258.4 24.4 %all-to-all-start.1 = ((bf16[64,8,512]{2,1,0:T(8,128)(2,1)}), bf16[64,8,512]{2,1,0:T(8,128)(2,1)S(1)}, u32[]{:S(2)}, u32[]{:S(2)}) async-start(bf16[64,8,512]{2,1,0:T(8,128)(2,1)} %convolution_convert_fusion.7), calls=%async_computation.1 | async-start | bytes 1048576 | tf_op jit(solution)/shard_map/all_to_all | solution.py:122
  282.9 9.6 copy-start.2
  282.9 23.8 %all-to-all-start.2 = ((bf16[64,8,512]{2,1,0:T(8,128)(2,1)}), bf16[64,8,512]{2,1,0:T(8,128)(2,1)}, u32[]{:S(2)}, u32[]{:S(2)}) async-start(bf16[64,8,512]{2,1,0:T(8,128)(2,1)} %convolution_convert_fusion.6), calls=%async_computation.2 | async-start | bytes 1048576 | tf_op jit(solution)/shard_map/all_to_all | solution.py:123
  379.9 23.2 %all-to-all-start.6 = ((bf16[64,2,2048]{2,1,0:T(2,128)(2,1)}), bf16[64,2,2048]{2,1,0:T(2,128)(2,1)S(1)}, u32[]{:S(2)}, u32[]{:S(2)}) async-start(bf16[64,2,2048]{2,1,0:T(2,128)(2,1)} %reshape.146), calls=%async_computation.6 | async-start | bytes 1048576 | tf_op jit(solution)/shard_map/all_to_all | solution.py:132
  403.1 22.9 %all-to-all-start.5 = ((bf16[64,2,2048]{2,1,0:T(2,128)(2,1)}), bf16[64,2,2048]{2,1,0:T(2,128)(2,1)}, u32[]{:S(2)}, u32[]{:S(2)}) async-start(bf16[64,2,2048]{2,1,0:T(2,128)(2,1)} %reshape.148), calls=%async_computation.5 | async-start | bytes 1048576 | tf_op jit(solution)/shard_map/all_to_all | solution.py:131
  426.1 22.4 %all-to-all-start.4 = ((bf16[64,2,2048]{2,1,0:T(2,128)(2,1)}), bf16[64,2,2048]{2,1,0:T(2,128)(2,1)S(1)}, u32[]{:S(2)}, u32[]{:S(2)}) async-start(bf16[64,2,2048]{2,1,0:T(2,128)(2,1)} %reshape.150), calls=%async_computation.4 | async-start | bytes 1048576 | tf_op jit(solution)/shard_map/all_to_all | solution.py:130
  432.6 47.0 %reduce-scatter.2.cloned.1.call-start = ((), (), s32[]{:S(2)}) async-start(), calls=%async_computation.9 | async-start | bytes 2621440 | tf_op jit(solution)/shard_map/reduce_scatter | solution.py:142
  450.2 2.0 copy-start.4
  450.2 2.0 copy-start.6
  450.2 2.0 copy-start.7
  453.9 0.7 copy-start.9
  453.9 726.9 %all-reduce.3.cloned.1.call-start = ((), (), s32[]{:S(2)}) async-start(), calls=%async_computation.10 | async-start | bytes 2097152
  455.8 1.3 copy-start.1
  457.1 24.8 %copy-start.5 = (bf16[1,512,512]{2,1,0:T(8,128)(2,1)S(1)}, bf16[1,512,512]{2,1,0:T(8,128)(2,1)}, u32[]{:S(2)}) copy-start(bf16[1,512,512]{2,1,0:T(8,128)(2,1)} %copy.94) | copy-start | bytes 1572868
  481.9 79.7 %copy-start.3 = (bf16[64,8,512]{2,1,0:T(8,128)(2,1)S(1)}, bf16[64,8,512]{2,1,0:T(8,128)(2,1)}, u32[]{:S(2)}) copy-start(bf16[64,8,512]{2,1,0:T(8,128)(2,1)} %param.7) | copy-start | bytes 1572868
Sparse Core Ops, SparseCore 0:
  193.2 31.0 all-gather.1
  454.0 25.5 reduce-scatter.1
  482.4 698.3 all-reduce.2
where the time goes:
time: 1190 us
  waiting for transfers between devices  728 us (61%)
  blocking collectives  260 us (22%)
  matrix products  75.3 us (6%)
  starting transfers between devices  55.3 us (5%)
  local copies, waits for them, and re-layouts  35.4 us (3%)
  other arithmetic  19.9 us (2%)
  between operations  14.7 us (1%)
    unnamed x4, waiting for transfers between devices  618 us
    all_gather x1, blocking collectives, shards(): w_part = lax.all_gather(weights, 'trk', axis=2, tiled=True)  184 us
    psum x1, blocking collectives, shards(): gain_sum = lax.psum(gain_term, ('grp', 'trk'))  76.2 us
  transfers between devices with their start and end apart: 10, of which 9 were waited for; matrix products, arithmetic and copies ran while one was open for 4% of the time, Pallas kernels for 0%

commit v1 on v0

--- a/solution.py
+++ b/solution.py
@@ -143,7 +143,7 @@
         raw_grad.astype(jnp.bfloat16), "grp", scatter_dimension=1, tiled=True
     ).astype(jnp.float32)
     summed_grad = lax.psum_scatter(partial_grad, "trk", scatter_dimension=2, tiled=True)
-    gain_sum = lax.psum(gain_term, ("grp", "trk"))
+    gain_sum = lax.psum(lax.psum(gain_term, "trk"), "grp")
     factor = float(cell_count) ** (-0.5)
     grad_fields = (upstream.astype(jnp.float32) + branch_cells.astype(jnp.float32)).astype(
         jnp.bfloat16

time: 1190 us -> 1190 us (level)
  blocking collectives: 260 us -> 370 us
  waiting for transfers between devices: 728 us -> 618 us
    unnamed x4, waiting for transfers between devices: 618 us -> 509 us
    psum x1 -> x2, blocking collectives: 76.2 us -> 186 us  [shards(): gain_sum = lax.psum(lax.psum(gain_term, 'trk'), 'grp')]
where the time goes in v1:
time: 1190 us
  waiting for transfers between devices  618 us (52%)
  blocking collectives  370 us (31%)
  matrix products  75.3 us (6%)
  starting transfers between devices  56.8 us (5%)
  local copies, waits for them, and re-layouts  35.4 us (3%)
  other arithmetic  20.7 us (2%)
  between operations  14.7 us (1%)
    unnamed x4, waiting for transfers between devices  509 us
    psum x2, blocking collectives, shards(): gain_sum = lax.psum(lax.psum(gain_term, 'trk'), 'grp')  186 us
    all_gather x1, blocking collectives, shards(): w_part = lax.all_gather(weights, 'trk', axis=2, tiled=True)  184 us
  transfers between devices with their start and end apart: 10, of which 9 were waited for; matrix products, arithmetic and copies ran while one was open for 4% of the time, Pallas kernels for 0%

profile of v1, /device:TPU:2, one launch (start us, length us, event | category | flops | bytes accessed | tf_op | source)
XLA Modules:
  0.0 1190.2 jit_solution(13712254902822985866)
XLA Ops:
  8.0 184.0 %all_gather.6 = bf16[4,128,512]{1,0,2:T(4,128)(2,1)S(1)} all-gather(bf16[4,128,8]{1,0,2:T(4,128)(2,1)S(1)} %copy.57), channel_id=1, replica_groups=mesh['grp'=4,'trk'=64] {'trk'}, dimensions={2}, use_global_device_ids=true | all-gather | bytes 532480 | tf_op jit(solution)/shard_map/all_gather | solution.py:112
  193.1 8.9 all-to-all-start.3
  202.5 21.9 %all-gather.2.cloned.1.call-done = bf16[4,512,512]{2,1,0:T(8,128)(2,1)} async-done(((bf16[4,128,512]{2,1,0:T(8,128)(2,1)}), bf16[4,512,512]{2,1,0:T(8,128)(2,1)}) %all-gather.2.cloned.1.call-update) | async-done | bytes 2097168 | tf_op jit(solution)/shard_map/all_gather | solution.py:113
  224.3 2.3 convolution_convert_fusion.8
  226.6 13.0 %all-to-all-start = ((bf16[64,8,512]{2,1,0:T(8,128)(2,1)}), bf16[64,8,512]{2,1,0:T(8,128)(2,1)S(1)}, u32[]{:S(2)}, u32[]{:S(2)}) async-start(bf16[64,8,512]{2,1,0:T(8,128)(2,1)} %convolution_convert_fusion.8), calls=%async_computation | async-start | bytes 1048576 | tf_op jit(solution)/shard_map/all_to_all | solution.py:121
  239.7 2.3 convolution_convert_fusion.7
  242.0 16.4 %all-to-all-done = bf16[64,8,512]{2,1,0:T(8,128)(2,1)S(1)} async-done(((bf16[64,8,512]{2,1,0:T(8,128)(2,1)}), bf16[64,8,512]{2,1,0:T(8,128)(2,1)S(1)}, u32[]{:S(2)}, u32[]{:S(2)}) %all-to-all-start) | async-done | bytes 524320 | tf_op jit(solution)/shard_map/all_to_all | solution.py:121
  258.4 6.5 all-to-all-start.1
  265.0 2.3 convolution_convert_fusion.6
  267.3 15.6 %all-to-all-done.1 = bf16[64,8,512]{2,1,0:T(8,128)(2,1)S(1)} async-done(((bf16[64,8,512]{2,1,0:T(8,128)(2,1)}), bf16[64,8,512]{2,1,0:T(8,128)(2,1)S(1)}, u32[]{:S(2)}, u32[]{:S(2)}) %all-to-all-start.1) | async-done | bytes 524320 | tf_op jit(solution)/shard_map/all_to_all | solution.py:122
  282.8 6.7 all-to-all-start.2
  293.1 2.4 reshape.122
  296.9 9.8 all-to-all-done.2
  306.7 2.4 reshape.124
  309.1 2.3 copy.62
  311.4 60.7 %while.16 = (s32[]{:T(128)}, bf16[8,512,64]{1,2,0:T(8,128)(2,1)}, bf16[8,512,64]{1,2,0:T(8,128)(2,1)}, bf16[8,512,64]{1,2,0:T(8,128)(2,1)}, bf16[8,512,64]{1,2,0...) while((s32[]{:T(128)}, bf16[8,512,64]{1,2,0:T(8,128)(2,1)}, ...), condition=%wide.region_6.7_spmd, body=%wide.region_2.6_spmd.sunk | while | flops 206699008 | bytes 11305061 | solution.py:78
  311.9 1.8 fusion.112
  317.2 1.8 fusion.109
  319.5 1.8 fusion.112
  324.8 1.8 fusion.109
  327.1 1.8 fusion.112
  332.3 1.8 fusion.109
  334.7 1.8 fusion.112
  342.3 1.8 fusion.112
  349.9 1.8 fusion.112
  357.4 1.8 fusion.112
  365.0 1.8 fusion.112
  372.1 2.4 copy.65
  375.1 3.8 reduce.1
  379.9 6.5 all-to-all-start.6
  387.3 3.8 reduce.2
  392.1 11.0 all-to-all-done.6
  403.1 6.5 all-to-all-start.5
  409.6 2.4 copy.63
  412.0 4.6 reduce.3
  416.7 2.0 reshape.150
  418.7 2.3 fusion.55
  421.5 4.5 all-to-all-done.5
  426.0 8.3 all-to-all-start.4
  436.0 3.6 reshape.149
  441.2 8.9 all-to-all-done.4
  451.8 2.0 fusion.58
  460.1 21.1 %reduce-scatter.2.cloned.1.call-done = bf16[4,128,512]{2,1,0:T(8,128)(2,1)} async-done(((bf16[4,512,512]{2,1,0:T(8,128)(2,1)}), bf16[4,128,512]{2,1,0:T(8,128)(2,1)}) %reduce-scatter.2.cloned.1.call-update) | async-done | bytes 524304 | tf_op jit(solution)/shard_map/reduce_scatter | solution.py:142
  481.2 2.3 copy.69
  483.5 2.8 fusion.64
  486.3 179.9 %psum.14 = f32[512]{0:T(512)S(1)} all-reduce(f32[512]{0:T(512)S(1)} %get-tuple-element.108), channel_id=1, replica_groups=mesh['grp'=4,'trk'=64] {'trk'}, use_global_device_ids=true, to_apply=%region_12.13 | all-reduce | flops 512 | bytes 4096 | tf_op jit(solution)/shard_map/psum | solution.py:146
  666.2 5.7 psum.15
  673.8 508.5 %all-reduce.3.cloned.1.call-done = f32[4,128,512]{1,0,2:T(4,128)} async-done(((f32[4,128,512]{1,0,2:T(4,128)}), f32[4,128,512]{1,0,2:T(4,128)}) %all-reduce.3.cloned.1.call-update) | async-done | bytes 1048592
  (119 shorter events, 65.3 us)
Async XLA Ops:
  7.2 194.8 %copy-start = (bf16[64,8,512]{2,1,0:T(8,128)(2,1)S(1)}, bf16[64,8,512]{2,1,0:T(8,128)(2,1)}, u32[]{:S(2)}) copy-start(bf16[64,8,512]{2,1,0:T(8,128)(2,1)} %param.6) | copy-start | bytes 1572868
  7.2 217.1 %all-gather.2.cloned.1.call-start = ((), (), s32[]{:S(2)}) async-start(), calls=%async_computation.8 | async-start | bytes 2621440 | tf_op jit(solution)/shard_map/all_gather | solution.py:113
  8.0 216.3 %copy-start.11 = (f32[512]{0:T(512)S(1)}, f32[512]{0:T(512)}, u32[]{:S(2)}) copy-start(f32[512]{0:T(512)} %param.8) | copy-start | bytes 6148
  193.1 33.6 %all-to-all-start.3 = ((bf16[64,8,512]{2,1,0:T(8,128)(2,1)}), bf16[64,8,512]{2,1,0:T(8,128)(2,1)S(1)}, u32[]{:S(2)}, u32[]{:S(2)}) async-start(bf16[64,8,512]{2,1,0:T(8,128)(2,1)} %param.7), calls=%async_computation.3 | async-start | bytes 1048576 | tf_op jit(solution)/shard_map/all_to_all | solution.py:124
  226.6 31.8 %all-to-all-start = ((bf16[64,8,512]{2,1,0:T(8,128)(2,1)}), bf16[64,8,512]{2,1,0:T(8,128)(2,1)S(1)}, u32[]{:S(2)}, u32[]{:S(2)}) async-start(bf16[64,8,512]{2,1,0:T(8,128)(2,1)} %convolution_convert_fusion.8), calls=%async_computation | async-start | bytes 1048576 | tf_op jit(solution)/shard_map/all_to_all | solution.py:121
  258.4 24.4 %all-to-all-start.1 = ((bf16[64,8,512]{2,1,0:T(8,128)(2,1)}), bf16[64,8,512]{2,1,0:T(8,128)(2,1)S(1)}, u32[]{:S(2)}, u32[]{:S(2)}) async-start(bf16[64,8,512]{2,1,0:T(8,128)(2,1)} %convolution_convert_fusion.7), calls=%async_computation.1 | async-start | bytes 1048576 | tf_op jit(solution)/shard_map/all_to_all | solution.py:122
  282.8 9.6 copy-start.3
  282.8 23.8 %all-to-all-start.2 = ((bf16[64,8,512]{2,1,0:T(8,128)(2,1)}), bf16[64,8,512]{2,1,0:T(8,128)(2,1)}, u32[]{:S(2)}, u32[]{:S(2)}) async-start(bf16[64,8,512]{2,1,0:T(8,128)(2,1)} %convolution_convert_fusion.6), calls=%async_computation.2 | async-start | bytes 1048576 | tf_op jit(solution)/shard_map/all_to_all | solution.py:123
  374.5 11.9 copy-start.6
  379.9 23.2 %all-to-all-start.6 = ((bf16[64,2,2048]{2,1,0:T(2,128)(2,1)}), bf16[64,2,2048]{2,1,0:T(2,128)(2,1)S(1)}, u32[]{:S(2)}, u32[]{:S(2)}) async-start(bf16[64,2,2048]{2,1,0:T(2,128)(2,1)} %reshape.146), calls=%async_computation.6 | async-start | bytes 1048576 | tf_op jit(solution)/shard_map/all_to_all | solution.py:132
  403.1 22.8 %all-to-all-start.5 = ((bf16[64,2,2048]{2,1,0:T(2,128)(2,1)}), bf16[64,2,2048]{2,1,0:T(2,128)(2,1)S(1)}, u32[]{:S(2)}, u32[]{:S(2)}) async-start(bf16[64,2,2048]{2,1,0:T(2,128)(2,1)} %reshape.148), calls=%async_computation.5 | async-start | bytes 1048576 | tf_op jit(solution)/shard_map/all_to_all | solution.py:131
  426.0 8.6 copy-start.2
  426.0 24.0 %all-to-all-start.4 = ((bf16[64,2,2048]{2,1,0:T(2,128)(2,1)}), bf16[64,2,2048]{2,1,0:T(2,128)(2,1)S(1)}, u32[]{:S(2)}, u32[]{:S(2)}) async-start(bf16[64,2,2048]{2,1,0:T(2,128)(2,1)} %reshape.150), calls=%async_computation.4 | async-start | bytes 1048576 | tf_op jit(solution)/shard_map/all_to_all | solution.py:130
  434.3 46.9 %reduce-scatter.2.cloned.1.call-start = ((), (), s32[]{:S(2)}) async-start(), calls=%async_computation.9 | async-start | bytes 2621440 | tf_op jit(solution)/shard_map/reduce_scatter | solution.py:142
  451.8 2.0 copy-start.5
  451.8 2.0 copy-start.9
  451.8 2.0 copy-start.10
  455.4 0.7 copy-start.12
  455.5 726.9 %all-reduce.3.cloned.1.call-start = ((), (), s32[]{:S(2)}) async-start(), calls=%async_computation.10 | async-start | bytes 2097152
  457.3 1.9 copy-start.1
  459.2 24.3 %copy-start.7 = (bf16[1,512,512]{2,1,0:T(8,128)(2,1)S(1)}, bf16[1,512,512]{2,1,0:T(8,128)(2,1)}, u32[]{:S(2)}) copy-start(bf16[1,512,512]{2,1,0:T(8,128)(2,1)} %copy.93) | copy-start | bytes 1572868
  459.2 24.3 %copy-start.8 = (bf16[1,512,512]{2,1,0:T(8,128)(2,1)S(1)}, bf16[1,512,512]{2,1,0:T(8,128)(2,1)}, u32[]{:S(2)}) copy-start(bf16[1,512,512]{2,1,0:T(8,128)(2,1)} %copy.94) | copy-start | bytes 1572868
  483.5 189.1 %copy-start.4 = (bf16[64,8,512]{2,1,0:T(8,128)(2,1)S(1)}, bf16[64,8,512]{2,1,0:T(8,128)(2,1)}, u32[]{:S(2)}) copy-start(bf16[64,8,512]{2,1,0:T(8,128)(2,1)} %param.7) | copy-start | bytes 1572868
Sparse Core Ops, SparseCore 0:
  193.2 31.0 all-gather.1
  455.6 25.5 reduce-scatter.1
  484.0 698.3 all-reduce.2
